TPU v7x, 32 devices: a whole 2x2x4 slice. The times are simulated.
32 devices in a mesh: rep: 4 (over y, x), shard: 8 (over z, core).
Axes of the slice: x: 2, y: 2, z: 4, core: 2. Of those that a mesh axis runs over, the one named last changes fastest.
Arguments:
- tokens: bfloat16 [4096, 768], P(('rep', 'shard')), may hold values from -6 to 6
- segment_ids: int32 [32, 128], P(('rep', 'shard')), may hold values from 0 to 3, never falling along the last dimension, each value on 1 to 64 neighbouring positions
- first_gain: bfloat16 [768], P('shard'), may hold values from 0.5 to 1.5
- first_shift: bfloat16 [768], P('shard'), may hold values from -3 to 3
- qkv_weight: bfloat16 [768, 2304], P('shard'), may hold values from -3 to 3, as said below
- qv_bias: bfloat16 [2, 768], P(None, 'shard'), may hold values from -3 to 3
- proj_weight: bfloat16 [768, 768], P('shard'), may hold values from -0.625 to 0.625
- proj_bias: bfloat16 [768], P('shard'), may hold values from -3 to 3
- second_gain: bfloat16 [768], P('shard'), may hold values from 0.5 to 1.5
- second_shift: bfloat16 [768], P('shard'), may hold values from -3 to 3
- fc_weight: bfloat16 [768, 3072], P('shard'), may hold values from -0.21875 to 0.21875
- fc_bias: bfloat16 [3072], P('shard'), may hold values from -3 to 3
- out_weight: bfloat16 [3072, 768], P('shard'), may hold values from -0.109375 to 0.109375
- out_bias: bfloat16 [768], P('shard'), may hold values from -3 to 3
- cotangent: bfloat16 [4096, 768], P(('rep', 'shard')), may hold values from -6 to 6
Outputs:
- block_output: bfloat16 [4096, 768], P(('rep', 'shard'))
- grad_tokens: float32 [4096, 768], P(('rep', 'shard'))
- grad_first_gain: float32 [768], P('shard')
- grad_first_shift: float32 [768], P('shard')
- grad_qkv_weight: float32 [768, 2304], P('shard')
- grad_qv_bias: float32 [2, 768], P(None, 'shard')
- grad_proj_weight: float32 [768, 768], P('shard')
- grad_proj_bias: float32 [768], P('shard')
- grad_second_gain: float32 [768], P('shard')
- grad_second_shift: float32 [768], P('shard')
- grad_fc_weight: float32 [768, 3072], P('shard')
- grad_fc_bias: float32 [3072], P('shard')
- grad_out_weight: float32 [3072, 768], P('shard')
- grad_out_bias: float32 [768], P('shard')
Inputs may be any that keep to these rules, and one draw needn't show every extreme that they name: `segment_ids`: each row holds 4 runs of equal numbers in rising order, each run 1 to 64 long, one of them exactly 64. `qkv_weight`: columns 0 to 767 project to queries, the next 768 columns to keys, the last 768 columns to values.
All inputs are finite; a program needn't handle non-finite values.
Results may differ from a plain program's by a relative error of at most 0.011.
Values may be sent and summed in bfloat16 or wider, within the bound.
A program may use at most 128 MiB of HBM per device.

v0:
```python
import math
import jax
import jax.numpy as jnp
from jax import lax
from jax.sharding import PartitionSpec as P

D = 768
HEADS = 12
HD = 64
FF = 3072
EPSILON = 1e-05


def layer_norm(field, norm_gain, norm_shift):
    center = field - jnp.mean(field, axis=-1, keepdims=True)
    spread = jnp.mean(center * center, axis=-1, keepdims=True)
    return center * lax.rsqrt(spread + EPSILON) * norm_gain + norm_shift


def gelu_tanh(field):
    return jax.nn.gelu(field, approximate=True)


def head_split(matrix):
    return matrix.reshape(matrix.shape[0], HEADS, HD)


def masked_scores(query, keys, segments):
    rows = query.shape[0]
    scores = jnp.einsum(
        "qhd,khd->hqk", head_split(query), head_split(keys), preferred_element_type=jnp.float32
    ) * (1.0 / math.sqrt(HD))
    position = lax.iota(jnp.int32, rows)
    allowed = (segments[:, None] == segments[None, :]) & (position[None, :] <= position[:, None])
    return jnp.where(allowed[None], scores, -1e30)


def attend_forward(query, keys, values, segments):
    rows = query.shape[0]
    scores = masked_scores(query, keys, segments)
    row_max = jnp.max(scores, axis=-1, keepdims=True)
    row_total = jnp.sum(jnp.exp(scores - row_max), axis=-1, keepdims=True)
    logsum = row_max + jnp.log(row_total)
    probs = jnp.exp(scores - logsum).astype(jnp.bfloat16)
    attended = jnp.einsum(
        "hqk,khd->qhd", probs, head_split(values), preferred_element_type=jnp.float32
    )
    return (attended.reshape(rows, D).astype(jnp.bfloat16), logsum)


def attend_backward(query, keys, values, segments, attended, logsum, grad_attended):
    rows = query.shape[0]
    scores = masked_scores(query, keys, segments)
    weights = jnp.exp(scores - logsum)
    grad_heads = head_split(grad_attended)
    grad_values = jnp.einsum(
        "hqk,qhd->khd", weights.astype(jnp.bfloat16), grad_heads, preferred_element_type=jnp.float32
    )
    grad_probs = jnp.einsum(
        "qhd,khd->hqk", grad_heads, head_split(values), preferred_element_type=jnp.float32
    )
    delta = jnp.einsum(
        "qhd,qhd->hq", grad_heads, head_split(attended), preferred_element_type=jnp.float32
    )
    grad_scores = (weights * (grad_probs - delta[..., None]) * (1.0 / math.sqrt(HD))).astype(
        jnp.bfloat16
    )
    grad_query = jnp.einsum(
        "hqk,khd->qhd", grad_scores, head_split(keys), preferred_element_type=jnp.float32
    )
    grad_keys = jnp.einsum(
        "hqk,qhd->khd", grad_scores, head_split(query), preferred_element_type=jnp.float32
    )
    return (grad_query.reshape(rows, D), grad_keys.reshape(rows, D), grad_values.reshape(rows, D))


def exchange(field, axis, split, concat):
    return lax.all_to_all(field, axis, split_axis=split, concat_axis=concat, tiled=True)


def spread(field, axis):
    parts = lax.axis_size(axis)
    return exchange(jnp.broadcast_to(field[None], (parts,) + field.shape), axis, 0, 0)


def by_replica(field, shards, reps):
    rows = field.shape[0]
    return field.reshape(shards, reps, rows // (shards * reps), -1).swapaxes(0, 1).reshape(rows, -1)


def per_device(
    tokens,
    segment_ids,
    first_gain,
    first_shift,
    qkv_weight,
    qv_bias,
    proj_weight,
    proj_bias,
    second_gain,
    second_shift,
    fc_weight,
    fc_bias,
    out_weight,
    out_bias,
    cotangent,
):
    low = jnp.bfloat16
    segments = segment_ids[0]
    own_rows = tokens.shape[0]
    shards = lax.axis_size("shard")
    reps = lax.axis_size("rep")
    factor = 1.0 / math.sqrt(own_rows * reps * shards)
    small = jnp.stack(
        [
            first_gain,
            first_shift,
            qv_bias[0],
            qv_bias[1],
            proj_bias,
            second_gain,
            second_shift,
            out_bias,
        ]
    )
    small_full = lax.all_gather(small, "shard", axis=1, tiled=True).astype(jnp.float32)
    gain_one, shift_one, q_bias, v_bias, proj_bias_full, gain_two, shift_two, out_bias_full = (
        small_full[i] for i in range(8)
    )
    qkv_full = lax.all_gather(qkv_weight, "shard", axis=0, tiled=True)
    proj_full = lax.all_gather(proj_weight, "shard", axis=0, tiled=True)
    fc_cols = exchange(fc_weight, "shard", 1, 0)
    inputs = tokens.astype(jnp.float32)
    normed_f, first_back = jax.vjp(layer_norm, inputs, gain_one, shift_one)
    normed_first = normed_f.astype(low)
    projected = jnp.dot(normed_first, qkv_full, preferred_element_type=jnp.float32)
    query = (projected[:, :D] + q_bias).astype(low)
    keys = projected[:, D : 2 * D].astype(low)
    values = (projected[:, 2 * D :] + v_bias).astype(low)
    attended, logsum = attend_forward(query, keys, values, segments)
    residual = (
        inputs + jnp.dot(attended, proj_full, preferred_element_type=jnp.float32) + proj_bias_full
    )
    cot_f = cotangent.astype(jnp.float32)
    normed_s, second_back = jax.vjp(layer_norm, residual, gain_two, shift_two)
    normed_all = lax.all_gather(normed_s.astype(low), "shard", axis=0, tiled=True)
    cot_later, normed_all = lax.optimization_barrier((cotangent, normed_all))
    cot_all = lax.all_gather(cot_later, "shard", axis=0, tiled=True)
    pre_act = jnp.dot(normed_all, fc_cols, preferred_element_type=jnp.float32) + fc_bias.astype(
        jnp.float32
    )
    activated, gelu_back = jax.vjp(gelu_tanh, pre_act)
    hidden = activated.astype(low)
    grad_hidden = jnp.dot(cot_all, out_weight.T, preferred_element_type=jnp.float32)
    (grad_pre,) = gelu_back(grad_hidden)
    grad_pre_low = grad_pre.astype(low)
    grad_normed_part = jnp.dot(grad_pre_low, fc_cols.T, preferred_element_type=jnp.float32).astype(
        low
    )
    grad_normed_low = lax.psum_scatter(grad_normed_part, "shard", scatter_dimension=0, tiled=True)
    term_out_weight = jnp.dot(hidden.T, cot_all, preferred_element_type=jnp.float32) * factor
    term_fc_weight = (
        jnp.dot(normed_all.T, grad_pre_low, preferred_element_type=jnp.float32) * factor
    )
    out_part = jnp.dot(hidden, out_weight, preferred_element_type=jnp.float32).astype(low)
    ff_terms = jnp.concatenate(
        [
            term_out_weight.astype(low).reshape(reps, -1, D),
            by_replica(term_fc_weight.astype(low), shards, reps).reshape(reps, -1, D),
        ],
        axis=1,
    )
    ff_sum = jnp.sum(exchange(ff_terms, "rep", 0, 0).astype(jnp.float32), axis=0).astype(low)
    first_later, attended_later, grad_normed_low, ff_sum = lax.optimization_barrier(
        (normed_first, attended, grad_normed_low, ff_sum)
    )
    first_all = lax.all_gather(first_later, "shard", axis=0, tiled=True)
    grad_normed_second = grad_normed_low.astype(jnp.float32)
    grad_from_norm, second_gain_sum, second_shift_sum = second_back(grad_normed_second)
    grad_residual = cot_f + grad_from_norm
    grad_residual_low = grad_residual.astype(low)
    grad_residual_all = lax.all_gather(grad_residual_low, "shard", axis=0, tiled=True)
    attended_cols = exchange(attended_later, "shard", 1, 0)
    grad_attended = jnp.dot(
        grad_residual_low, proj_full.T, preferred_element_type=jnp.float32
    ).astype(low)
    out_rows = out_weight.shape[0] // reps
    out_piece = ff_sum[:out_rows]
    fc_piece = ff_sum[out_rows:].reshape(D // reps, -1)
    fc_piece = exchange(fc_piece, "shard", 0, 1)
    ff_all = spread(jnp.concatenate([out_piece, fc_piece.reshape(-1, D)]), "rep").astype(
        jnp.float32
    )
    grad_query, grad_keys, grad_values = attend_backward(
        query, keys, values, segments, attended, logsum, grad_attended
    )
    grad_projected = jnp.concatenate([grad_query, grad_keys, grad_values], axis=1).astype(low)
    grad_projected, ff_all = lax.optimization_barrier((grad_projected, ff_all))
    out_grad = ff_all[:, :out_rows].reshape(-1, D)
    fc_grad = ff_all[:, out_rows:].reshape(-1, FF)
    grad_cols = exchange(grad_projected, "shard", 1, 0)
    grad_normed_first = jnp.dot(grad_projected, qkv_full.T, preferred_element_type=jnp.float32)
    out_later, grad_cols = lax.optimization_barrier((out_part, grad_cols))
    out_sum = lax.psum_scatter(out_later, "shard", scatter_dimension=0, tiled=True)
    result = (residual + out_sum.astype(jnp.float32) + out_bias_full).astype(low)
    term_qkv_weight = jnp.dot(first_all.T, grad_cols, preferred_element_type=jnp.float32) * factor
    term_proj_weight = (
        jnp.dot(attended_cols.T, grad_residual_all, preferred_element_type=jnp.float32) * factor
    )
    attn_terms = jnp.concatenate(
        [
            term_proj_weight.astype(low).reshape(reps, -1, D),
            by_replica(term_qkv_weight.astype(low), shards, reps).reshape(reps, -1, D),
        ],
        axis=1,
    )
    attn_sum = jnp.sum(exchange(attn_terms, "rep", 0, 0).astype(jnp.float32), axis=0).astype(low)
    proj_rows = proj_weight.shape[0] // reps
    proj_piece = attn_sum[:proj_rows]
    qkv_piece = attn_sum[proj_rows:].reshape(D // reps, -1)
    qkv_piece = exchange(qkv_piece, "shard", 0, 1)
    attn_all = spread(jnp.concatenate([proj_piece, qkv_piece.reshape(-1, D)]), "rep").astype(
        jnp.float32
    )
    proj_grad = attn_all[:, :proj_rows].reshape(-1, D)
    qkv_grad = attn_all[:, proj_rows:].reshape(-1, 3 * D)
    grad_input_norm, first_gain_sum, first_shift_sum = first_back(grad_normed_first)
    grad_inputs = grad_residual + grad_input_norm
    terms = jnp.stack(
        [
            first_gain_sum,
            first_shift_sum,
            jnp.sum(grad_query, axis=0),
            jnp.sum(grad_values, axis=0),
            jnp.sum(grad_residual, axis=0),
            second_gain_sum,
            second_shift_sum,
            jnp.sum(cot_f, axis=0),
        ]
    )
    count = terms.shape[0]
    terms = terms.reshape(count, shards, -1).swapaxes(0, 1).reshape(shards, -1)
    own_terms = jnp.concatenate(
        [jnp.sum(exchange(terms, "shard", 0, 0), axis=0), jnp.sum(grad_pre, axis=0)]
    )
    sums = jnp.sum(spread(own_terms, "rep"), axis=0) * factor
    own_cols = D // shards
    fc_bias_grad = sums[count * own_cols :]
    sums = sums[: count * own_cols].reshape(count, own_cols)
    return (
        result,
        grad_inputs,
        sums[0],
        sums[1],
        qkv_grad,
        sums[2:4],
        proj_grad,
        sums[4],
        sums[5],
        sums[6],
        fc_grad,
        fc_bias_grad,
        out_grad,
        sums[7],
    )


def solution(mesh):
    return jax.shard_map(
        per_device,
        mesh=mesh,
        in_specs=(
            P(("rep", "shard"), None),
            P(("rep", "shard"), None),
            P("shard"),
            P("shard"),
            P("shard", None),
            P(None, "shard"),
            P("shard", None),
            P("shard"),
            P("shard"),
            P("shard"),
            P("shard", None),
            P("shard"),
            P("shard", None),
            P("shard"),
            P(("rep", "shard"), None),
        ),
        out_specs=(
            P(("rep", "shard"), None),
            P(("rep", "shard"), None),
            P("shard"),
            P("shard"),
            P("shard", None),
            P(None, "shard"),
            P("shard", None),
            P("shard"),
            P("shard"),
            P("shard"),
            P("shard", None),
            P("shard"),
            P("shard", None),
            P("shard"),
        ),
        check_vma=False,
    )
```

profile of v0, /device:TPU:0, one launch (start us, length us, event | category | flops | bytes accessed | tf_op | source)
XLA Modules:
  0.0 345.6 jit_solution(11735301634824392414)
XLA Ops:
  11.7 14.5 %all-gather = bf16[8,96,8]{1,2,0:T(8,128)(2,1)S(1)} all-gather(bf16[1,96,8]{1,2,0:T(8,128)(2,1)S(1)} %bitcast.133), channel_id=1, replica_groups=mesh['rep'=4,'shard'=8] {'shard'}, dimensions={0}, use_global_device_ids=true | all-gather | bytes 13824 | tf_op jit(solution)/shard_map/all_gather | solution.py:126
  28.9 25.1 %all-gather.8.cloned.1.call-done = bf16[768,2304]{1,0:T(8,128)(2,1)} async-done(((bf16[96,2304]{1,0:T(8,128)(2,1)}), bf16[768,2304]{1,0:T(8,128)(2,1)}) %all-gather.8.cloned.1.call-update) | async-done | bytes 3538960 | tf_op jit(solution)/shard_map/all_gather | solution.py:130
  53.9 2.6 fusion.57
  58.0 19.2 %all-gather.10.cloned.1.call-done = bf16[768,768]{1,0:T(8,128)(2,1)} async-done(((bf16[96,768]{1,0:T(8,128)(2,1)}), bf16[768,768]{1,0:T(8,128)(2,1)}) %all-gather.10.cloned.1.call-update) | async-done | bytes 1179664 | tf_op jit(solution)/shard_map/all_gather | solution.py:131
  77.2 1.8 fusion.56
  80.6 24.9 %all-gather.12.cloned.1.call-done = bf16[1024,768]{1,0:T(8,128)(2,1)} async-done(((bf16[128,768]{1,0:T(8,128)(2,1)}), bf16[1024,768]{1,0:T(8,128)(2,1)}) %all-gather.12.cloned.1.call-update) | async-done | bytes 1572880 | tf_op jit(solution)/shard_map/all_gather | solution.py:146
  106.4 3.5 %all-to-all-start = ((bf16[96,8,384]{2,0,1:T(8,128)(2,1)}), bf16[96,8,384]{2,0,1:T(8,128)(2,1)S(1)}, u32[]{:S(2)}, u32[]{:S(2)}) async-start(bf16[96,8,384]{2,0,1:T(8,128)(2,1)} %bitcast.106), calls=%async_computation | async-start | bytes 1179648 | tf_op jit(solution)/shard_map/all_to_all | solution.py:78
  110.0 30.8 %all-gather.14.cloned.1.call-done = bf16[1024,768]{1,0:T(8,128)(2,1)} async-done(((bf16[128,768]{1,0:T(8,128)(2,1)}), bf16[1024,768]{1,0:T(8,128)(2,1)}) %all-gather.14.cloned.1.call-update) | async-done | bytes 1572880 | tf_op jit(solution)/shard_map/all_gather | solution.py:148
  140.8 3.6 %fusion.58 = f32[1024,384]{1,0:T(8,128)} fusion(bf16[1024,768]{1,0:T(8,128)(2,1)} %all-gather.14.cloned.1.call-done, bf16[384,768]{1,0:T(8,128)(2,1)S(1)} %copy-done), kind=kOutput, calls=%fused_computation.119 | convolution fusion | flops 603979776 | bytes 3735552 | tf_op jit(solution)/shard_map/dot_general | solution.py:154
  144.4 5.6 %fusion.47 = (f32[384]{0:T(512)}, bf16[1024,384]{1,0:T(8,128)(2,1)S(1)}, f32[1024,384]{1,0:T(8,128)}) fusion(f32[1024,384]{1,0:T(8,128)} %fusion.58, f32[384]{0:T(512)S(1)} %convert_element_type.103, bf16[1024,768]{1,0:T(8,128)(2,1)} %all-gather.12.cloned.1.call-done, bf16[768,384]{1,0:T(8,128)(2,1)S(1)} %bitcast.125), kind=kOutput, calls=%fused_computation.109 | convolution fusion | flops 612630144 | bytes 6097920 | tf_op jit(solution)/shard_map/dot_general | solution.py:149
  150.9 2.2 convolution_convert_fusion
  153.1 2.6 fusion.7
  156.0 2.8 fusion.6
  158.9 19.4 %all_to_all.125 = bf16[4,192,768]{2,1,0:T(8,128)(2,1)S(1)} all-to-all(bf16[4,192,768]{2,1,0:T(8,128)(2,1)S(1)} %pad_maximum_fusion), channel_id=1, replica_groups=mesh['rep'=4,'shard'=8] {'rep'}, dimensions={0} | all-to-all | bytes 2359296 | tf_op jit(solution)/shard_map/all_to_all | solution.py:78
  179.2 7.8 %reduce-scatter.3.cloned.1.call-done = bf16[128,768]{1,0:T(8,128)(2,1)} async-done(((bf16[1024,768]{1,0:T(8,128)(2,1)}), bf16[128,768]{1,0:T(8,128)(2,1)}) %reduce-scatter.3.cloned.1.call-update) | async-done | bytes 196624 | tf_op jit(solution)/shard_map/reduce_scatter | solution.py:160
  187.1 1.7 fusion.53
  188.8 1.7 all_to_all.93
  190.5 4.0 %all-to-all-start.2 = ((bf16[8,24,384]{2,1,0:T(8,128)(2,1)}), bf16[8,24,384]{2,1,0:T(8,128)(2,1)}, u32[]{:S(2)}, u32[]{:S(2)}) async-start(bf16[8,24,384]{2,1,0:T(8,128)(2,1)} %all_to_all.93), calls=%async_computation.3 | async-start | bytes 294912 | tf_op jit(solution)/shard_map/all_to_all | solution.py:78
  194.6 1.8 fusion.30
  199.8 2.1 convolution_convert_fusion.3
  203.6 1.9 all-to-all-done.2
  207.6 4.6 %all-to-all-start.3 = ((bf16[4,192,768]{2,1,0:T(8,128)(2,1)}), bf16[4,192,768]{2,1,0:T(8,128)(2,1)}, u32[]{:S(2)}, u32[]{:S(2)}) async-start(bf16[4,192,768]{2,1,0:T(8,128)(2,1)} %broadcast_in_dim.34), calls=%async_computation.4 | async-start | bytes 2359296 | tf_op jit(solution)/shard_map/all_to_all | solution.py:78
  215.4 11.7 %all-to-all-done.3 = bf16[4,192,768]{2,1,0:T(8,128)(2,1)} async-done(((bf16[4,192,768]{2,1,0:T(8,128)(2,1)}), bf16[4,192,768]{2,1,0:T(8,128)(2,1)}, u32[]{:S(2)}, u32[]{:S(2)}) %all-to-all-start.3) | async-done | bytes 1179680 | tf_op jit(solution)/shard_map/all_to_all | solution.py:78
  227.1 1.5 convert_element_type.115
  228.6 4.2 %all-to-all-start.4 = ((bf16[128,8,288]{0,2,1:T(8,128)(2,1)}), bf16[128,8,288]{0,2,1:T(8,128)(2,1)}, u32[]{:S(2)}, u32[]{:S(2)}) async-start(bf16[128,8,288]{0,2,1:T(8,128)(2,1)} %bitcast.107), calls=%async_computation.5 | async-start | bytes 1179648 | tf_op jit(solution)/shard_map/all_to_all | solution.py:78
  232.8 3.8 %convolution_convert_fusion.1 = bf16[1024,768]{1,0:T(8,128)(2,1)} fusion(bf16[384,768]{1,0:T(8,128)(2,1)S(1)} %copy-done, f32[1024,384]{1,0:T(8,128)} %get-tuple-element.76), kind=kOutput, calls=%fused_computation.3 | convolution fusion | flops 608305152 | bytes 3735552 | tf_op jit(solution)/shard_map/dot_general | solution.py:165
  240.7 12.3 %all-to-all-done.4 = bf16[128,8,288]{0,2,1:T(8,128)(2,1)} async-done(((bf16[128,8,288]{0,2,1:T(8,128)(2,1)}), bf16[128,8,288]{0,2,1:T(8,128)(2,1)}, u32[]{:S(2)}, u32[]{:S(2)}) %all-to-all-start.4) | async-done | bytes 589856 | tf_op jit(solution)/shard_map/all_to_all | solution.py:78
  253.0 4.2 %all-to-all-start.7 = ((bf16[128,8,96]{0,2,1:T(8,128)(2,1)}), bf16[128,8,96]{0,2,1:T(8,128)(2,1)}, u32[]{:S(2)}, u32[]{:S(2)}) async-start(bf16[128,8,96]{0,2,1:T(8,128)(2,1)} %bitcast.109), calls=%async_computation.9 | async-start | bytes 393216 | tf_op jit(solution)/shard_map/all_to_all | solution.py:78
  257.2 2.0 copy_bitcast_fusion
  259.3 4.2 %fusion.46 = (f32[768]{0:T(1024)}, f32[128]{0:T(128)S(1)}, f32[128,768]{1,0:T(8,128)S(1)}) fusion(f32[768]{0:T(1024)S(1)} %get-tuple-element.50, f32[128]{0:T(128)S(1)} %copy-done.20, bf16[128,768]{1,0:T(8,128)(2,1)S(1)} %copy-done.1, bf16[128,2304]{0,1:T(8,128)(2,1)} %pad_maximum_fusion.1, bf16[768,2304]{1,0:T(8,128)(2,1)} %all-gather.8.cloned.1.call-done), kind=kOutput, calls=%fused_computation.108 | convolution fusion | flops 453573760 | bytes 4725760 | tf_op jit(solution)/shard_map/dot_general | solution.py:202
  267.3 3.0 fusion.11
  270.3 2.1 copy.150
  272.4 1.9 copy.151
  274.4 2.8 reshape_reshape.7
  277.1 5.0 %all-to-all-start.5 = ((f32[8,1,768]{2,1,0:T(1,128)}), f32[8,1,768]{2,1,0:T(1,128)S(1)}, u32[]{:S(2)}, u32[]{:S(2)}) async-start(f32[8,1,768]{2,1,0:T(1,128)} %all_to_all.113), calls=%async_computation.7 | async-start | bytes 49152 | tf_op jit(solution)/shard_map/all_to_all | solution.py:78
  282.1 2.0 fusion.14
  285.0 3.0 all-to-all-done.5
  288.0 4.2 %all-to-all-start.8 = ((bf16[4,96,768]{2,1,0:T(8,128)(2,1)}), bf16[4,96,768]{2,1,0:T(8,128)(2,1)}, u32[]{:S(2)}, u32[]{:S(2)}) async-start(bf16[4,96,768]{2,1,0:T(8,128)(2,1)} %pad_maximum_fusion.2), calls=%async_computation.10 | async-start | bytes 1179648 | tf_op jit(solution)/shard_map/all_to_all | solution.py:78
  292.3 9.2 %all-to-all-done.8 = bf16[4,96,768]{2,1,0:T(8,128)(2,1)} async-done(((bf16[4,96,768]{2,1,0:T(8,128)(2,1)}), bf16[4,96,768]{2,1,0:T(8,128)(2,1)}, u32[]{:S(2)}, u32[]{:S(2)}) %all-to-all-start.8) | async-done | bytes 589856 | tf_op jit(solution)/shard_map/all_to_all | solution.py:78
  302.1 3.3 all-to-all-start.6
  307.1 1.8 all_to_all.109
  310.0 4.0 %all-to-all-start.9 = ((bf16[8,24,288]{2,1,0:T(8,128)(2,1)}), bf16[8,24,288]{2,1,0:T(8,128)(2,1)}, u32[]{:S(2)}, u32[]{:S(2)}) async-start(bf16[8,24,288]{2,1,0:T(8,128)(2,1)} %all_to_all.109), calls=%async_computation.11 | async-start | bytes 294912 | tf_op jit(solution)/shard_map/all_to_all | solution.py:78
  314.0 1.7 fusion.50
  315.7 2.5 reshape.296
  318.3 2.8 all-to-all-done.9
  323.1 3.5 %all-to-all-start.10 = ((bf16[4,96,768]{2,1,0:T(8,128)(2,1)}), bf16[4,96,768]{2,1,0:T(8,128)(2,1)S(1)}, u32[]{:S(2)}, u32[]{:S(2)}) async-start(bf16[4,96,768]{2,1,0:T(8,128)(2,1)} %broadcast_in_dim.68), calls=%async_computation.12 | async-start | bytes 1179648 | tf_op jit(solution)/shard_map/all_to_all | solution.py:78
  328.5 6.6 %all-to-all-done.10 = bf16[4,96,768]{2,1,0:T(8,128)(2,1)S(1)} async-done(((bf16[4,96,768]{2,1,0:T(8,128)(2,1)}), bf16[4,96,768]{2,1,0:T(8,128)(2,1)S(1)}, u32[]{:S(2)}, u32[]{:S(2)}) %all-to-all-start.10) | async-done | bytes 589856 | tf_op jit(solution)/shard_map/all_to_all | solution.py:78
  337.1 1.7 add_convert_fusion
  (168 shorter events, 41.7 us)
Async XLA Ops:
  7.2 133.6 %copy-start = (bf16[384,768]{1,0:T(8,128)(2,1)S(1)}, bf16[384,768]{1,0:T(8,128)(2,1)}, u32[]{:S(2)}) copy-start(bf16[384,768]{1,0:T(8,128)(2,1)} %param.27) | copy-start | bytes 1769476
  7.2 46.7 %all-gather.8.cloned.1.call-start = ((), (), s32[]{:S(2)}) async-start(), calls=%async_computation.13 | async-start | bytes 3981312 | tf_op jit(solution)/shard_map/all_gather | solution.py:130
  7.9 69.2 %all-gather.10.cloned.1.call-start = ((), (), s32[]{:S(2)}) async-start(), calls=%async_computation.14 | async-start | bytes 1327104 | tf_op jit(solution)/shard_map/all_gather | solution.py:131
  8.7 96.8 %all-gather.12.cloned.1.call-start = ((), (), s32[]{:S(2)}) async-start(), calls=%async_computation.15 | async-start | bytes 1769472 | tf_op jit(solution)/shard_map/all_gather | solution.py:146
  9.8 46.8 %copy-start.19 = (f32[128]{0:T(128)}, f32[128]{0:T(128)S(1)}, u32[]{:S(2)}) copy-start(f32[128]{0:T(128)S(1)} %broadcast_multiply_fusion.2) | copy-start | bytes 1540
  10.9 45.7 %copy-start.23 = (f32[128]{0:T(128)}, f32[128]{0:T(128)S(1)}, u32[]{:S(2)}) copy-start(f32[128]{0:T(128)S(1)} %fusion.41) | copy-start | bytes 1540
  28.9 27.7 %copy-start.6 = (bf16[128,768]{1,0:T(8,128)(2,1)}, bf16[128,768]{1,0:T(8,128)(2,1)S(1)}, u32[]{:S(2)}) copy-start(bf16[128,768]{1,0:T(8,128)(2,1)S(1)} %fusion.25) | copy-start | bytes 589828
  56.9 1.1 copy-start.9
  57.1 0.9 copy-start.7
  57.2 19.9 %copy-start.1 = (bf16[128,768]{1,0:T(8,128)(2,1)S(1)}, bf16[128,768]{1,0:T(8,128)(2,1)}, u32[]{:S(2)}) copy-start(bf16[128,768]{1,0:T(8,128)(2,1)} %param.15) | copy-start | bytes 589828
  58.0 145.1 %copy-start.5 = (bf16[12,64,128]{2,1,0:T(8,128)(2,1)}, bf16[12,64,128]{2,1,0:T(8,128)(2,1)S(1)}, u32[]{:S(2)}) copy-start(bf16[12,64,128]{2,1,0:T(8,128)(2,1)S(1)} %convolution_convert_fusion.4) | copy-start | bytes 589828
  77.2 28.4 %copy-start.14 = (bf16[96,3072]{1,0:T(8,128)(2,1)S(1)}, bf16[96,3072]{1,0:T(8,128)(2,1)}, u32[]{:S(2)}) copy-start(bf16[96,3072]{1,0:T(8,128)(2,1)} %param.25) | copy-start | bytes 1769476
  78.9 27.5 %copy-start.22 = (f32[128]{0:T(128)}, f32[128]{0:T(128)S(1)}, u32[]{:S(2)}) copy-start(f32[128]{0:T(128)S(1)} %broadcast_multiply_fusion.1) | copy-start | bytes 1540
  79.2 27.2 %copy-start.25 = (f32[128]{0:T(128)}, f32[128]{0:T(128)S(1)}, u32[]{:S(2)}) copy-start(f32[128]{0:T(128)S(1)} %fusion.42) | copy-start | bytes 1540
  79.7 30.3 %copy-start.29 = (bf16[384]{0:T(512)(128)(2,1)S(1)}, bf16[384]{0:T(512)(128)(2,1)}, u32[]{:S(2)}) copy-start(bf16[384]{0:T(512)(128)(2,1)} %param.26) | copy-start | bytes 2308
  80.5 60.3 %all-gather.14.cloned.1.call-start = ((), (), s32[]{:S(2)}) async-start(), calls=%async_computation.16 | async-start | bytes 1769472 | tf_op jit(solution)/shard_map/all_gather | solution.py:148
  106.4 38.0 %all-to-all-start = ((bf16[96,8,384]{2,0,1:T(8,128)(2,1)}), bf16[96,8,384]{2,0,1:T(8,128)(2,1)S(1)}, u32[]{:S(2)}, u32[]{:S(2)}) async-start(bf16[96,8,384]{2,0,1:T(8,128)(2,1)} %bitcast.106), calls=%async_computation | async-start | bytes 1179648 | tf_op jit(solution)/shard_map/all_to_all | solution.py:78
  110.0 77.1 %reduce-scatter.3.cloned.1.call-start = ((), (), s32[]{:S(2)}) async-start(), calls=%async_computation.17 | async-start | bytes 1769472 | tf_op jit(solution)/shard_map/reduce_scatter | solution.py:160
  150.0 0.9 copy-start.33
  153.1 114.3 %all-gather.18.cloned.1.call-start = ((), (), s32[]{:S(2)}) async-start(), calls=%async_computation.20 | async-start | bytes 1769472 | tf_op jit(solution)/shard_map/all_gather | solution.py:177
  188.8 11.0 %copy-start.2 = (bf16[768,768]{1,0:T(8,128)(2,1)S(1)}, bf16[768,768]{1,0:T(8,128)(2,1)}, u32[]{:S(2)}) copy-start(bf16[768,768]{1,0:T(8,128)(2,1)} %all-gather.10.cloned.1.call-done) | copy-start | bytes 3538948
  190.5 14.9 %all-to-all-start.2 = ((bf16[8,24,384]{2,1,0:T(8,128)(2,1)}), bf16[8,24,384]{2,1,0:T(8,128)(2,1)}, u32[]{:S(2)}, u32[]{:S(2)}) async-start(bf16[8,24,384]{2,1,0:T(8,128)(2,1)} %all_to_all.93), calls=%async_computation.3 | async-start | bytes 294912 | tf_op jit(solution)/shard_map/all_to_all | solution.py:78
  194.5 87.6 %all-gather.16.cloned.1.call-start = ((), (), s32[]{:S(2)}) async-start(), calls=%async_computation.19 | async-start | bytes 1769472 | tf_op jit(solution)/shard_map/all_gather | solution.py:182
  194.6 4.4 %copy-start.12 = (bf16[128,768]{1,0:T(8,128)(2,1)S(1)}, bf16[128,768]{1,0:T(8,128)(2,1)}, u32[]{:S(2)}) copy-start(bf16[128,768]{1,0:T(8,128)(2,1)} %param.29) | copy-start | bytes 589828
  202.0 4.5 %copy-start.15 = (bf16[96,768]{1,0:T(8,128)(2,1)S(1)}, bf16[96,768]{1,0:T(8,128)(2,1)}, u32[]{:S(2)}) copy-start(bf16[96,768]{1,0:T(8,128)(2,1)} %get-tuple-element.64) | copy-start | bytes 442372
  206.5 5.7 %copy-start.10 = (bf16[128,768]{0,1:T(8,128)(2,1)S(1)}, bf16[128,768]{0,1:T(8,128)(2,1)}, u32[]{:S(2)}) copy-start(bf16[128,768]{0,1:T(8,128)(2,1)} %copy-done.9) | copy-start | bytes 589828
  207.6 5.0 %copy-start.8 = (bf16[128,768]{0,1:T(8,128)(2,1)S(1)}, bf16[128,768]{0,1:T(8,128)(2,1)}, u32[]{:S(2)}) copy-start(bf16[128,768]{0,1:T(8,128)(2,1)} %copy-done.7) | copy-start | bytes 589828
  207.6 19.6 %all-to-all-start.3 = ((bf16[4,192,768]{2,1,0:T(8,128)(2,1)}), bf16[4,192,768]{2,1,0:T(8,128)(2,1)}, u32[]{:S(2)}, u32[]{:S(2)}) async-start(bf16[4,192,768]{2,1,0:T(8,128)(2,1)} %broadcast_in_dim.34), calls=%async_computation.4 | async-start | bytes 2359296 | tf_op jit(solution)/shard_map/all_to_all | solution.py:78
  228.6 24.4 %all-to-all-start.4 = ((bf16[128,8,288]{0,2,1:T(8,128)(2,1)}), bf16[128,8,288]{0,2,1:T(8,128)(2,1)}, u32[]{:S(2)}, u32[]{:S(2)}) async-start(bf16[128,8,288]{0,2,1:T(8,128)(2,1)} %bitcast.107), calls=%async_computation.5 | async-start | bytes 1179648 | tf_op jit(solution)/shard_map/all_to_all | solution.py:78
  232.8 5.2 %copy-start.18 = (f32[768]{0:T(1024)S(1)}, f32[768]{0:T(1024)}, u32[]{:S(2)}) copy-start(f32[768]{0:T(1024)} %get-tuple-element.42) | copy-start | bytes 9220
  232.8 7.2 %copy-start.16 = (f32[12,64]{1,0:T(8,128)S(1)}, f32[12,64]{1,0:T(8,128)}, u32[]{:S(2)}) copy-start(f32[12,64]{1,0:T(8,128)} %get-tuple-element.62) | copy-start | bytes 9220
  253.0 6.2 %copy-start.20 = (f32[128]{0:T(128)S(1)}, f32[128]{0:T(128)}, u32[]{:S(2)}) copy-start(f32[128]{0:T(128)} %copy-done.19) | copy-start | bytes 1540
  253.0 24.1 %all-to-all-start.7 = ((bf16[128,8,96]{0,2,1:T(8,128)(2,1)}), bf16[128,8,96]{0,2,1:T(8,128)(2,1)}, u32[]{:S(2)}, u32[]{:S(2)}) async-start(bf16[128,8,96]{0,2,1:T(8,128)(2,1)} %bitcast.109), calls=%async_computation.9 | async-start | bytes 393216 | tf_op jit(solution)/shard_map/all_to_all | solution.py:78
  257.1 79.9 %reduce-scatter.5.cloned.1.call-start = ((), (), s32[]{:S(2)}) async-start(), calls=%async_computation.18 | async-start | bytes 1769472 | tf_op jit(solution)/shard_map/reduce_scatter | solution.py:204
  259.2 4.3 %copy-start.31 = (f32[128]{0:T(128)S(1)}, f32[128]{0:T(128)}, u32[]{:S(2)}) copy-start(f32[128]{0:T(128)} %copy-done.30) | copy-start | bytes 1540
  259.2 4.3 %copy-start.24 = (f32[128]{0:T(128)S(1)}, f32[128]{0:T(128)}, u32[]{:S(2)}) copy-start(f32[128]{0:T(128)} %copy-done.23) | copy-start | bytes 1540
  259.2 4.6 %copy-start.4 = (f32[128,768]{1,0:T(8,128)S(1)}, f32[128,768]{1,0:T(8,128)}, u32[]{:S(2)}) copy-start(f32[128,768]{1,0:T(8,128)} %copy-done.3) | copy-start | bytes 1179652
  259.2 4.6 %copy-start.13 = (bf16[128,768]{1,0:T(8,128)(2,1)S(1)}, bf16[128,768]{1,0:T(8,128)(2,1)}, u32[]{:S(2)}) copy-start(bf16[128,768]{1,0:T(8,128)(2,1)} %param.29) | copy-start | bytes 589828
  259.2 4.6 %copy-start.21 = (f32[128]{0:T(128)S(1)}, f32[128]{0:T(128)}, u32[]{:S(2)}) copy-start(f32[128]{0:T(128)} %copy-done.19) | copy-start | bytes 1540
  259.2 4.6 %copy-start.28 = (f32[128]{0:T(128)S(1)}, f32[128]{0:T(128)}, u32[]{:S(2)}) copy-start(f32[128]{0:T(128)} %copy-done.27) | copy-start | bytes 1540
  277.1 10.9 %all-to-all-start.5 = ((f32[8,1,768]{2,1,0:T(1,128)}), f32[8,1,768]{2,1,0:T(1,128)S(1)}, u32[]{:S(2)}, u32[]{:S(2)}) async-start(f32[8,1,768]{2,1,0:T(1,128)} %all_to_all.113), calls=%async_computation.7 | async-start | bytes 49152 | tf_op jit(solution)/shard_map/all_to_all | solution.py:78
  282.1 2.0 copy-start.11
  284.1 8.1 %copy-start.26 = (f32[384]{0:T(512)S(1)}, f32[384]{0:T(512)}, u32[]{:S(2)}) copy-start(f32[384]{0:T(512)} %get-tuple-element.51) | copy-start | bytes 4612
  288.0 13.4 %all-to-all-start.8 = ((bf16[4,96,768]{2,1,0:T(8,128)(2,1)}), bf16[4,96,768]{2,1,0:T(8,128)(2,1)}, u32[]{:S(2)}, u32[]{:S(2)}) async-start(bf16[4,96,768]{2,1,0:T(8,128)(2,1)} %pad_maximum_fusion.2), calls=%async_computation.10 | async-start | bytes 1179648 | tf_op jit(solution)/shard_map/all_to_all | solution.py:78
  302.1 7.9 %all-to-all-start.6 = ((f32[4,1,1152]{2,1,0:T(1,128)}), f32[4,1,1152]{2,1,0:T(1,128)S(1)}, u32[]{:S(2)}, u32[]{:S(2)}) async-start(f32[4,1,1152]{2,1,0:T(1,128)} %broadcast_in_dim.37), calls=%async_computation.8 | async-start | bytes 36864 | tf_op jit(solution)/shard_map/all_to_all | solution.py:78
  310.0 11.0 %all-to-all-start.9 = ((bf16[8,24,288]{2,1,0:T(8,128)(2,1)}), bf16[8,24,288]{2,1,0:T(8,128)(2,1)}, u32[]{:S(2)}, u32[]{:S(2)}) async-start(bf16[8,24,288]{2,1,0:T(8,128)(2,1)} %all_to_all.109), calls=%async_computation.11 | async-start | bytes 294912 | tf_op jit(solution)/shard_map/all_to_all | solution.py:78
  323.1 12.0 %all-to-all-start.10 = ((bf16[4,96,768]{2,1,0:T(8,128)(2,1)}), bf16[4,96,768]{2,1,0:T(8,128)(2,1)S(1)}, u32[]{:S(2)}, u32[]{:S(2)}) async-start(bf16[4,96,768]{2,1,0:T(8,128)(2,1)} %broadcast_in_dim.68), calls=%async_computation.12 | async-start | bytes 1179648 | tf_op jit(solution)/shard_map/all_to_all | solution.py:78
  335.2 1.9 copy-start.17
  (4 other events, 2.8 us)
Sparse Core Ops, SparseCore 0:
  9.7 44.2 all-gather.7
  55.6 21.5 all-gather.9
  80.6 24.8 all-gather.11
  107.0 33.7 all-gather.13
  153.2 33.8 reduce-scatter.2
  188.6 26.5 all-gather.17
  217.4 27.5 all-gather.15
  260.3 35.7 reduce-scatter.4
where the time goes:
time: 347 us; the launch traced here: 346 us
  waiting for transfers between devices  158 us (46%)
  starting transfers between devices  40.7 us (12%)
  local copies, waits for them, and re-layouts  40.4 us (12%)
  matrix products  39.6 us (11%)
  blocking collectives  33.9 us (10%)
  other arithmetic  18.2 us (5%)
  between operations  14.9 us (4%)
    all_to_all x10, waiting for transfers between devices, exchange(): lax.all_to_all(field, axis, split_axis=split, concat_axis=concat, tiled=T...  48.6 us
    all_to_all x10, starting transfers between devices, exchange(): lax.all_to_all(field, axis, split_axis=split, concat_axis=concat, tiled=T...  40.4 us
    all_gather x1, waiting for transfers between devices, per_device(): cot_all = lax.all_gather(cot_later, 'shard', axis=0, tiled=True)  30.8 us
    all_gather x1, waiting for transfers between devices, per_device(): qkv_full = lax.all_gather(qkv_weight, 'shard', axis=0, tiled=True)  25.1 us
    all_gather x1, waiting for transfers between devices, per_device(): lax.all_gather(normed_s.astype(low), 'shard', axis=0, tiled=True)  24.9 us
    all_to_all x1, blocking collectives, exchange(): lax.all_to_all(field, axis, split_axis=split, concat_axis=concat, tiled=T...  19.4 us
    all_gather x1, waiting for transfers between devices, per_device(): proj_full = lax.all_gather(proj_weight, 'shard', axis=0, tiled=True)  19.2 us
    all_gather x1, blocking collectives, per_device(): lax.all_gather(small, 'shard', axis=1, tiled=True).astype(jnp.float32)  14.5 us
  transfers between devices with their start and end apart: 18, of which 13 were waited for; matrix products, arithmetic and copies ran while one was open for 23% of the time, Pallas kernels for 0%

commit v1 on v0

--- a/solution.py
+++ b/solution.py
@@ -9,6 +9,12 @@
 HD = 64
 FF = 3072
 EPSILON = 1e-05
+
+
+def shape_pieces_all(local_block, mat, ax_name):
+    earlier = jnp.concatenate([local_block, mat], 1)
+    aux = lax.all_gather(earlier, axis_name=ax_name, axis=0, tiled=True)
+    return jnp.split(aux, [local_block.shape[1]], 1)
 
 
 def layer_norm(field, norm_gain, norm_shift):
@@ -127,8 +133,7 @@
     gain_one, shift_one, q_bias, v_bias, proj_bias_full, gain_two, shift_two, out_bias_full = (
         small_full[i] for i in range(8)
     )
-    qkv_full = lax.all_gather(qkv_weight, "shard", axis=0, tiled=True)
-    proj_full = lax.all_gather(proj_weight, "shard", axis=0, tiled=True)
+    qkv_full, proj_full = shape_pieces_all(qkv_weight, proj_weight, "shard")
     fc_cols = exchange(fc_weight, "shard", 1, 0)
     inputs = tokens.astype(jnp.float32)
     normed_f, first_back = jax.vjp(layer_norm, inputs, gain_one, shift_one)

time: 347 us -> 336 us (0.968)
  waiting for transfers between devices: 158 us -> 153 us
  local copies, waits for them, and re-layouts: 40.4 us -> 36.2 us
    all_gather x2 -> x1, waiting for transfers between devices: 44.2 us -> 39.4 us  [shape_pieces_all(): aux = lax.all_gather(earlier, axis_name=ax_name, axis=0, tiled=True)]
  transfers between devices with their start and end apart: 18 -> 17, of which waited for: 13 -> 12; matrix products, arithmetic and copies ran while one was open for 23% -> 20% of each run, Pallas kernels for 0% -> 0%
where the time goes in v1:
time: 336 us; the launch traced here: 334 us
  waiting for transfers between devices  153 us (46%)
  starting transfers between devices  41.7 us (12%)
  matrix products  39.5 us (12%)
  local copies, waits for them, and re-layouts  36.2 us (11%)
  blocking collectives  33.8 us (10%)
  other arithmetic  15.2 us (5%)
  between operations  15 us (4%)
    all_to_all x10, waiting for transfers between devices, exchange(): lax.all_to_all(field, axis, split_axis=split, concat_axis=concat, tiled=T...  51.2 us
    all_to_all x10, starting transfers between devices, exchange(): lax.all_to_all(field, axis, split_axis=split, concat_axis=concat, tiled=T...  41.4 us
    all_gather x1, waiting for transfers between devices, shape_pieces_all(): aux = lax.all_gather(earlier, axis_name=ax_name, axis=0, tiled=True)  39.4 us
    all_gather x1, waiting for transfers between devices, per_device(): cot_all = lax.all_gather(cot_later, 'shard', axis=0, tiled=True)  30.8 us
    all_gather x1, waiting for transfers between devices, per_device(): lax.all_gather(normed_s.astype(low), 'shard', axis=0, tiled=True)  24 us
    all_to_all x1, blocking collectives, exchange(): lax.all_to_all(field, axis, split_axis=split, concat_axis=concat, tiled=T...  19.4 us
    all_gather x1, blocking collectives, per_device(): lax.all_gather(small, 'shard', axis=1, tiled=True).astype(jnp.float32)  14.4 us
    reduce_scatter x1, waiting for transfers between devices, per_device(): lax.psum_scatter(grad_normed_part, 'shard', scatter_dimension=0, tiled=True)  7.55 us
  transfers between devices with their start and end apart: 17, of which 12 were waited for; matrix products, arithmetic and copies ran while one was open for 20% of the time, Pallas kernels for 0%

profile of v1, /device:TPU:0, one launch (start us, length us, event | category | flops | bytes accessed | tf_op | source)
XLA Modules:
  0.0 334.4 jit_solution(2015553096293627685)
XLA Ops:
  7.3 2.1 pad_maximum_fusion.1
  9.6 14.4 %all-gather = bf16[8,96,8]{1,2,0:T(8,128)(2,1)S(1)} all-gather(bf16[1,96,8]{1,2,0:T(8,128)(2,1)S(1)} %bitcast.130), channel_id=1, replica_groups=mesh['rep'=4,'shard'=8] {'shard'}, dimensions={0}, use_global_device_ids=true | all-gather | bytes 13824 | tf_op jit(solution)/shard_map/all_gather | solution.py:132
  25.3 39.4 %all-gather.7.cloned.1.call-done = bf16[768,3072]{1,0:T(8,128)(2,1)} async-done(((bf16[96,3072]{1,0:T(8,128)(2,1)}), bf16[768,3072]{1,0:T(8,128)(2,1)}) %all-gather.7.cloned.1.call-update) | async-done | bytes 4718608 | tf_op jit(solution)/shard_map/all_gather | solution.py:16
  64.8 2.6 fusion.2
  68.8 1.8 fusion.62
  72.3 24.0 %all-gather.9.cloned.1.call-done = bf16[1024,768]{1,0:T(8,128)(2,1)} async-done(((bf16[128,768]{1,0:T(8,128)(2,1)}), bf16[1024,768]{1,0:T(8,128)(2,1)}) %all-gather.9.cloned.1.call-update) | async-done | bytes 1572880 | tf_op jit(solution)/shard_map/all_gather | solution.py:151
  97.2 3.5 %all-to-all-start = ((bf16[96,8,384]{2,0,1:T(8,128)(2,1)}), bf16[96,8,384]{2,0,1:T(8,128)(2,1)S(1)}, u32[]{:S(2)}, u32[]{:S(2)}) async-start(bf16[96,8,384]{2,0,1:T(8,128)(2,1)} %bitcast.102), calls=%async_computation | async-start | bytes 1179648 | tf_op jit(solution)/shard_map/all_to_all | solution.py:84
  100.8 30.8 %all-gather.11.cloned.1.call-done = bf16[1024,768]{1,0:T(8,128)(2,1)} async-done(((bf16[128,768]{1,0:T(8,128)(2,1)}), bf16[1024,768]{1,0:T(8,128)(2,1)}) %all-gather.11.cloned.1.call-update) | async-done | bytes 1572880 | tf_op jit(solution)/shard_map/all_gather | solution.py:153
  131.6 3.6 %fusion.63 = f32[1024,384]{1,0:T(8,128)} fusion(bf16[1024,768]{1,0:T(8,128)(2,1)} %all-gather.11.cloned.1.call-done, bf16[384,768]{1,0:T(8,128)(2,1)S(1)} %copy-done), kind=kOutput, calls=%fused_computation.125 | convolution fusion | flops 603979776 | bytes 3735552 | tf_op jit(solution)/shard_map/dot_general | solution.py:159
  135.1 5.5 %fusion.53 = (f32[384]{0:T(512)}, bf16[1024,384]{1,0:T(8,128)(2,1)S(1)}, f32[1024,384]{1,0:T(8,128)}) fusion(f32[1024,384]{1,0:T(8,128)} %fusion.63, f32[384]{0:T(512)S(1)} %convert_element_type.103, bf16[1024,768]{1,0:T(8,128)(2,1)} %all-gather.9.cloned.1.call-done, bf16[768,384]{1,0:T(8,128)(2,1)S(1)} %bitcast.121), kind=kOutput, calls=%fused_computation.116 | convolution fusion | flops 612630144 | bytes 6097920 | tf_op jit(solution)/shard_map/dot_general | solution.py:154
  141.6 2.2 convolution_convert_fusion
  143.9 2.6 fusion.11
  146.8 2.8 fusion.10
  149.7 19.4 %all_to_all.125 = bf16[4,192,768]{2,1,0:T(8,128)(2,1)S(1)} all-to-all(bf16[4,192,768]{2,1,0:T(8,128)(2,1)S(1)} %pad_maximum_fusion), channel_id=1, replica_groups=mesh['rep'=4,'shard'=8] {'rep'}, dimensions={0} | all-to-all | bytes 2359296 | tf_op jit(solution)/shard_map/all_to_all | solution.py:84
  170.0 7.5 %reduce-scatter.3.cloned.1.call-done = bf16[128,768]{1,0:T(8,128)(2,1)} async-done(((bf16[1024,768]{1,0:T(8,128)(2,1)}), bf16[128,768]{1,0:T(8,128)(2,1)}) %reduce-scatter.3.cloned.1.call-update) | async-done | bytes 196624 | tf_op jit(solution)/shard_map/reduce_scatter | solution.py:165
  179.4 3.4 %all-to-all-start.2 = ((bf16[8,24,384]{2,1,0:T(8,128)(2,1)}), bf16[8,24,384]{2,1,0:T(8,128)(2,1)S(1)}, u32[]{:S(2)}, u32[]{:S(2)}) async-start(bf16[8,24,384]{2,1,0:T(8,128)(2,1)} %all_to_all.93), calls=%async_computation.3 | async-start | bytes 294912 | tf_op jit(solution)/shard_map/all_to_all | solution.py:84
  182.8 1.8 fusion.36
  186.4 1.9 convolution_convert_fusion.3
  189.0 1.6 all-to-all-done.2
  191.8 5.1 %all-to-all-start.3 = ((bf16[4,192,768]{2,1,0:T(8,128)(2,1)}), bf16[4,192,768]{2,1,0:T(8,128)(2,1)}, u32[]{:S(2)}, u32[]{:S(2)}) async-start(bf16[4,192,768]{2,1,0:T(8,128)(2,1)} %broadcast_in_dim.34), calls=%async_computation.4 | async-start | bytes 2359296 | tf_op jit(solution)/shard_map/all_to_all | solution.py:84
  200.1 10.5 %all-to-all-done.3 = bf16[4,192,768]{2,1,0:T(8,128)(2,1)} async-done(((bf16[4,192,768]{2,1,0:T(8,128)(2,1)}), bf16[4,192,768]{2,1,0:T(8,128)(2,1)}, u32[]{:S(2)}, u32[]{:S(2)}) %all-to-all-start.3) | async-done | bytes 1179680 | tf_op jit(solution)/shard_map/all_to_all | solution.py:84
  210.6 1.5 convert_element_type.115
  212.1 5.4 %all-to-all-start.4 = ((bf16[128,8,288]{0,2,1:T(8,128)(2,1)}), bf16[128,8,288]{0,2,1:T(8,128)(2,1)}, u32[]{:S(2)}, u32[]{:S(2)}) async-start(bf16[128,8,288]{0,2,1:T(8,128)(2,1)} %bitcast.108), calls=%async_computation.5 | async-start | bytes 1179648 | tf_op jit(solution)/shard_map/all_to_all | solution.py:84
  217.5 3.8 %convolution_convert_fusion.1 = bf16[1024,768]{1,0:T(8,128)(2,1)} fusion(bf16[384,768]{1,0:T(8,128)(2,1)S(1)} %copy-done, f32[1024,384]{1,0:T(8,128)} %get-tuple-element.76), kind=kOutput, calls=%fused_computation.7 | convolution fusion | flops 608305152 | bytes 3735552 | tf_op jit(solution)/shard_map/dot_general | solution.py:170
  221.3 1.3 stack.61
  223.3 1.4 stack.59
  225.4 16.4 %all-to-all-done.4 = bf16[128,8,288]{0,2,1:T(8,128)(2,1)} async-done(((bf16[128,8,288]{0,2,1:T(8,128)(2,1)}), bf16[128,8,288]{0,2,1:T(8,128)(2,1)}, u32[]{:S(2)}, u32[]{:S(2)}) %all-to-all-start.4) | async-done | bytes 589856 | tf_op jit(solution)/shard_map/all_to_all | solution.py:84
  241.8 4.1 %all-to-all-start.7 = ((bf16[128,8,96]{0,2,1:T(8,128)(2,1)}), bf16[128,8,96]{0,2,1:T(8,128)(2,1)}, u32[]{:S(2)}, u32[]{:S(2)}) async-start(bf16[128,8,96]{0,2,1:T(8,128)(2,1)} %bitcast.104), calls=%async_computation.9 | async-start | bytes 393216 | tf_op jit(solution)/shard_map/all_to_all | solution.py:84
  246.0 2.0 copy_bitcast_fusion
  248.1 4.2 %fusion.52 = (f32[768]{0:T(1024)}, f32[128]{0:T(128)S(1)}, f32[128,768]{1,0:T(8,128)S(1)}) fusion(f32[768]{0:T(1024)S(1)} %get-tuple-element.50, f32[128]{0:T(128)S(1)} %copy-done.19, bf16[128,768]{1,0:T(8,128)(2,1)S(1)} %copy-done.1, bf16[128,2304]{0,1:T(8,128)(2,1)} %pad_maximum_fusion.2, bf16[768,3072]{1,0:T(8,128)(2,1)} %all-gather.7.cloned.1.call-done), kind=kOutput, calls=%fused_computation.115 | convolution fusion | flops 453573760 | bytes 4725760 | tf_op jit(solution)/shard_map/dot_general | solution.py:207
  256.2 3.0 fusion.15
  259.2 2.1 copy.150
  261.2 1.9 copy.151
  263.2 2.8 reshape_reshape.7
  265.9 5.0 %all-to-all-start.5 = ((f32[8,1,768]{2,1,0:T(1,128)}), f32[8,1,768]{2,1,0:T(1,128)S(1)}, u32[]{:S(2)}, u32[]{:S(2)}) async-start(f32[8,1,768]{2,1,0:T(1,128)} %all_to_all.113), calls=%async_computation.7 | async-start | bytes 49152 | tf_op jit(solution)/shard_map/all_to_all | solution.py:84
  270.9 2.0 fusion.18
  273.8 3.1 all-to-all-done.5
  276.9 4.2 %all-to-all-start.8 = ((bf16[4,96,768]{2,1,0:T(8,128)(2,1)}), bf16[4,96,768]{2,1,0:T(8,128)(2,1)}, u32[]{:S(2)}, u32[]{:S(2)}) async-start(bf16[4,96,768]{2,1,0:T(8,128)(2,1)} %pad_maximum_fusion.3), calls=%async_computation.10 | async-start | bytes 1179648 | tf_op jit(solution)/shard_map/all_to_all | solution.py:84
  281.2 9.1 %all-to-all-done.8 = bf16[4,96,768]{2,1,0:T(8,128)(2,1)} async-done(((bf16[4,96,768]{2,1,0:T(8,128)(2,1)}), bf16[4,96,768]{2,1,0:T(8,128)(2,1)}, u32[]{:S(2)}, u32[]{:S(2)}) %all-to-all-start.8) | async-done | bytes 589856 | tf_op jit(solution)/shard_map/all_to_all | solution.py:84
  290.9 3.3 all-to-all-start.6
  295.9 1.8 all_to_all.109
  298.8 4.0 %all-to-all-start.9 = ((bf16[8,24,288]{2,1,0:T(8,128)(2,1)}), bf16[8,24,288]{2,1,0:T(8,128)(2,1)}, u32[]{:S(2)}, u32[]{:S(2)}) async-start(bf16[8,24,288]{2,1,0:T(8,128)(2,1)} %all_to_all.109), calls=%async_computation.11 | async-start | bytes 294912 | tf_op jit(solution)/shard_map/all_to_all | solution.py:84
  302.8 1.6 fusion.56
  304.5 2.5 reshape.296
  307.0 2.8 all-to-all-done.9
  311.9 3.5 %all-to-all-start.10 = ((bf16[4,96,768]{2,1,0:T(8,128)(2,1)}), bf16[4,96,768]{2,1,0:T(8,128)(2,1)S(1)}, u32[]{:S(2)}, u32[]{:S(2)}) async-start(bf16[4,96,768]{2,1,0:T(8,128)(2,1)} %broadcast_in_dim.68), calls=%async_computation.12 | async-start | bytes 1179648 | tf_op jit(solution)/shard_map/all_to_all | solution.py:84
  317.3 6.6 %all-to-all-done.10 = bf16[4,96,768]{2,1,0:T(8,128)(2,1)S(1)} async-done(((bf16[4,96,768]{2,1,0:T(8,128)(2,1)}), bf16[4,96,768]{2,1,0:T(8,128)(2,1)S(1)}, u32[]{:S(2)}, u32[]{:S(2)}) %all-to-all-start.10) | async-done | bytes 589856 | tf_op jit(solution)/shard_map/all_to_all | solution.py:84
  325.9 1.7 add_convert_fusion
  (186 shorter events, 31.7 us)
Async XLA Ops:
  7.2 124.4 %copy-start = (bf16[384,768]{1,0:T(8,128)(2,1)S(1)}, bf16[384,768]{1,0:T(8,128)(2,1)}, u32[]{:S(2)}) copy-start(bf16[384,768]{1,0:T(8,128)(2,1)} %param.27) | copy-start | bytes 1769476
  7.2 2.3 copy-start.42
  7.3 17.4 %copy-start.1 = (bf16[128,768]{1,0:T(8,128)(2,1)S(1)}, bf16[128,768]{1,0:T(8,128)(2,1)}, u32[]{:S(2)}) copy-start(bf16[128,768]{1,0:T(8,128)(2,1)} %param.15) | copy-start | bytes 589828
  7.3 17.8 %copy-start.28 = (s32[1,128]{1,0:T(1,128)S(1)}, s32[1,128]{1,0:T(1,128)}, u32[]{:S(2)}) copy-start(s32[1,128]{1,0:T(1,128)} %param.16) | copy-start | bytes 1540
  7.3 57.5 %all-gather.7.cloned.1.call-start = ((), (), s32[]{:S(2)}) async-start(), calls=%async_computation.13 | async-start | bytes 5308416 | tf_op jit(solution)/shard_map/all_gather | solution.py:16
  9.4 86.8 %all-gather.9.cloned.1.call-start = ((), (), s32[]{:S(2)}) async-start(), calls=%async_computation.14 | async-start | bytes 1769472 | tf_op jit(solution)/shard_map/all_gather | solution.py:151
  24.8 42.6 %copy-start.18 = (f32[128]{0:T(128)}, f32[128]{0:T(128)S(1)}, u32[]{:S(2)}) copy-start(f32[128]{0:T(128)S(1)} %broadcast_multiply_fusion.2) | copy-start | bytes 1540
  25.0 42.4 %copy-start.32 = (f32[128]{0:T(128)}, f32[128]{0:T(128)S(1)}, u32[]{:S(2)}) copy-start(f32[128]{0:T(128)S(1)} %fusion.34) | copy-start | bytes 1540
  25.0 42.4 %copy-start.23 = (f32[128]{0:T(128)}, f32[128]{0:T(128)S(1)}, u32[]{:S(2)}) copy-start(f32[128]{0:T(128)S(1)} %fusion.47) | copy-start | bytes 1540
  25.3 42.1 %copy-start.5 = (bf16[128,768]{1,0:T(8,128)(2,1)}, bf16[128,768]{1,0:T(8,128)(2,1)S(1)}, u32[]{:S(2)}) copy-start(bf16[128,768]{1,0:T(8,128)(2,1)S(1)} %fusion.31) | copy-start | bytes 589828
  68.8 119.7 %copy-start.4 = (bf16[12,64,128]{2,1,0:T(8,128)(2,1)}, bf16[12,64,128]{2,1,0:T(8,128)(2,1)S(1)}, u32[]{:S(2)}) copy-start(bf16[12,64,128]{2,1,0:T(8,128)(2,1)S(1)} %convolution_convert_fusion.4) | copy-start | bytes 589828
  68.8 27.4 %copy-start.14 = (bf16[96,3072]{1,0:T(8,128)(2,1)S(1)}, bf16[96,3072]{1,0:T(8,128)(2,1)}, u32[]{:S(2)}) copy-start(bf16[96,3072]{1,0:T(8,128)(2,1)} %param.25) | copy-start | bytes 1769476
  70.7 26.5 %copy-start.21 = (f32[128]{0:T(128)}, f32[128]{0:T(128)S(1)}, u32[]{:S(2)}) copy-start(f32[128]{0:T(128)S(1)} %broadcast_multiply_fusion.1) | copy-start | bytes 1540
  70.9 26.3 %copy-start.25 = (f32[128]{0:T(128)}, f32[128]{0:T(128)S(1)}, u32[]{:S(2)}) copy-start(f32[128]{0:T(128)S(1)} %fusion.48) | copy-start | bytes 1540
  71.4 29.4 %copy-start.31 = (bf16[384]{0:T(512)(128)(2,1)S(1)}, bf16[384]{0:T(512)(128)(2,1)}, u32[]{:S(2)}) copy-start(bf16[384]{0:T(512)(128)(2,1)} %param.26) | copy-start | bytes 2308
  72.2 59.3 %all-gather.11.cloned.1.call-start = ((), (), s32[]{:S(2)}) async-start(), calls=%async_computation.15 | async-start | bytes 1769472 | tf_op jit(solution)/shard_map/all_gather | solution.py:153
  97.2 38.0 %all-to-all-start = ((bf16[96,8,384]{2,0,1:T(8,128)(2,1)}), bf16[96,8,384]{2,0,1:T(8,128)(2,1)S(1)}, u32[]{:S(2)}, u32[]{:S(2)}) async-start(bf16[96,8,384]{2,0,1:T(8,128)(2,1)} %bitcast.102), calls=%async_computation | async-start | bytes 1179648 | tf_op jit(solution)/shard_map/all_to_all | solution.py:84
  100.7 76.9 %reduce-scatter.3.cloned.1.call-start = ((), (), s32[]{:S(2)}) async-start(), calls=%async_computation.16 | async-start | bytes 1769472 | tf_op jit(solution)/shard_map/reduce_scatter | solution.py:165
  143.8 112.3 %all-gather.15.cloned.1.call-start = ((), (), s32[]{:S(2)}) async-start(), calls=%async_computation.19 | async-start | bytes 1769472 | tf_op jit(solution)/shard_map/all_gather | solution.py:182
  170.0 14.6 %copy-start.35 = (f32[128]{0:T(128)S(1)}, f32[128]{0:T(128)}, u32[]{:S(2)}) copy-start(f32[128]{0:T(128)} %copy-done.34) | copy-start | bytes 1540
  170.0 14.6 %copy-start.22 = (f32[128]{0:T(128)S(1)}, f32[128]{0:T(128)}, u32[]{:S(2)}) copy-start(f32[128]{0:T(128)} %copy-done.21) | copy-start | bytes 1540
  170.0 14.6 %copy-start.26 = (f32[128]{0:T(128)S(1)}, f32[128]{0:T(128)}, u32[]{:S(2)}) copy-start(f32[128]{0:T(128)} %copy-done.25) | copy-start | bytes 1540
  170.0 15.6 %copy-start.11 = (bf16[128,768]{1,0:T(8,128)(2,1)S(1)}, bf16[128,768]{1,0:T(8,128)(2,1)}, u32[]{:S(2)}) copy-start(bf16[128,768]{1,0:T(8,128)(2,1)} %param.29) | copy-start | bytes 589828
  177.6 7.1 %copy-start.13 = (bf16[128,768]{1,0:T(8,128)(2,1)S(1)}, bf16[128,768]{1,0:T(8,128)(2,1)}, u32[]{:S(2)}) copy-start(bf16[128,768]{1,0:T(8,128)(2,1)} %reduce-scatter.3.cloned.1.call-done) | copy-start | bytes 589828
  179.4 11.2 %all-to-all-start.2 = ((bf16[8,24,384]{2,1,0:T(8,128)(2,1)}), bf16[8,24,384]{2,1,0:T(8,128)(2,1)S(1)}, u32[]{:S(2)}, u32[]{:S(2)}) async-start(bf16[8,24,384]{2,1,0:T(8,128)(2,1)} %all_to_all.93), calls=%async_computation.3 | async-start | bytes 294912 | tf_op jit(solution)/shard_map/all_to_all | solution.py:84
  182.8 88.2 %all-gather.13.cloned.1.call-start = ((), (), s32[]{:S(2)}) async-start(), calls=%async_computation.18 | async-start | bytes 1769472 | tf_op jit(solution)/shard_map/all_gather | solution.py:187
  184.9 3.6 %copy-start.29 = (f32[128]{0:T(128)}, f32[128]{0:T(128)S(1)}, u32[]{:S(2)}) copy-start(f32[128]{0:T(128)S(1)} %negate_multiply_fusion.1) | copy-start | bytes 1540
  190.7 6.2 %copy-start.9 = (bf16[128,768]{0,1:T(8,128)(2,1)S(1)}, bf16[128,768]{0,1:T(8,128)(2,1)}, u32[]{:S(2)}) copy-start(bf16[128,768]{0,1:T(8,128)(2,1)} %copy-done.8) | copy-start | bytes 589828
  191.8 5.4 %copy-start.7 = (bf16[128,768]{0,1:T(8,128)(2,1)S(1)}, bf16[128,768]{0,1:T(8,128)(2,1)}, u32[]{:S(2)}) copy-start(bf16[128,768]{0,1:T(8,128)(2,1)} %copy-done.6) | copy-start | bytes 589828
  191.8 18.8 %all-to-all-start.3 = ((bf16[4,192,768]{2,1,0:T(8,128)(2,1)}), bf16[4,192,768]{2,1,0:T(8,128)(2,1)}, u32[]{:S(2)}, u32[]{:S(2)}) async-start(bf16[4,192,768]{2,1,0:T(8,128)(2,1)} %broadcast_in_dim.34), calls=%async_computation.4 | async-start | bytes 2359296 | tf_op jit(solution)/shard_map/all_to_all | solution.py:84
  212.1 29.7 %all-to-all-start.4 = ((bf16[128,8,288]{0,2,1:T(8,128)(2,1)}), bf16[128,8,288]{0,2,1:T(8,128)(2,1)}, u32[]{:S(2)}, u32[]{:S(2)}) async-start(bf16[128,8,288]{0,2,1:T(8,128)(2,1)} %bitcast.108), calls=%async_computation.5 | async-start | bytes 1179648 | tf_op jit(solution)/shard_map/all_to_all | solution.py:84
  217.5 5.2 %copy-start.17 = (f32[768]{0:T(1024)S(1)}, f32[768]{0:T(1024)}, u32[]{:S(2)}) copy-start(f32[768]{0:T(1024)} %get-tuple-element.42) | copy-start | bytes 9220
  217.5 7.2 %copy-start.15 = (f32[12,64]{1,0:T(8,128)S(1)}, f32[12,64]{1,0:T(8,128)}, u32[]{:S(2)}) copy-start(f32[12,64]{1,0:T(8,128)} %get-tuple-element.62) | copy-start | bytes 9220
  241.8 6.2 %copy-start.19 = (f32[128]{0:T(128)S(1)}, f32[128]{0:T(128)}, u32[]{:S(2)}) copy-start(f32[128]{0:T(128)} %copy-done.18) | copy-start | bytes 1540
  241.8 24.1 %all-to-all-start.7 = ((bf16[128,8,96]{0,2,1:T(8,128)(2,1)}), bf16[128,8,96]{0,2,1:T(8,128)(2,1)}, u32[]{:S(2)}, u32[]{:S(2)}) async-start(bf16[128,8,96]{0,2,1:T(8,128)(2,1)} %bitcast.104), calls=%async_computation.9 | async-start | bytes 393216 | tf_op jit(solution)/shard_map/all_to_all | solution.py:84
  245.9 79.9 %reduce-scatter.5.cloned.1.call-start = ((), (), s32[]{:S(2)}) async-start(), calls=%async_computation.17 | async-start | bytes 1769472 | tf_op jit(solution)/shard_map/reduce_scatter | solution.py:209
  248.0 4.3 %copy-start.33 = (f32[128]{0:T(128)S(1)}, f32[128]{0:T(128)}, u32[]{:S(2)}) copy-start(f32[128]{0:T(128)} %copy-done.32) | copy-start | bytes 1540
  248.0 4.3 %copy-start.24 = (f32[128]{0:T(128)S(1)}, f32[128]{0:T(128)}, u32[]{:S(2)}) copy-start(f32[128]{0:T(128)} %copy-done.23) | copy-start | bytes 1540
  248.0 4.6 %copy-start.3 = (f32[128,768]{1,0:T(8,128)S(1)}, f32[128,768]{1,0:T(8,128)}, u32[]{:S(2)}) copy-start(f32[128,768]{1,0:T(8,128)} %copy-done.2) | copy-start | bytes 1179652
  248.0 4.6 %copy-start.12 = (bf16[128,768]{1,0:T(8,128)(2,1)S(1)}, bf16[128,768]{1,0:T(8,128)(2,1)}, u32[]{:S(2)}) copy-start(bf16[128,768]{1,0:T(8,128)(2,1)} %param.29) | copy-start | bytes 589828
  248.0 4.6 %copy-start.20 = (f32[128]{0:T(128)S(1)}, f32[128]{0:T(128)}, u32[]{:S(2)}) copy-start(f32[128]{0:T(128)} %copy-done.18) | copy-start | bytes 1540
  248.0 4.6 %copy-start.30 = (f32[128]{0:T(128)S(1)}, f32[128]{0:T(128)}, u32[]{:S(2)}) copy-start(f32[128]{0:T(128)} %copy-done.29) | copy-start | bytes 1540
  265.9 11.0 %all-to-all-start.5 = ((f32[8,1,768]{2,1,0:T(1,128)}), f32[8,1,768]{2,1,0:T(1,128)S(1)}, u32[]{:S(2)}, u32[]{:S(2)}) async-start(f32[8,1,768]{2,1,0:T(1,128)} %all_to_all.113), calls=%async_computation.7 | async-start | bytes 49152 | tf_op jit(solution)/shard_map/all_to_all | solution.py:84
  272.9 8.2 %copy-start.27 = (f32[384]{0:T(512)S(1)}, f32[384]{0:T(512)}, u32[]{:S(2)}) copy-start(f32[384]{0:T(512)} %get-tuple-element.51) | copy-start | bytes 4612
  276.9 13.3 %all-to-all-start.8 = ((bf16[4,96,768]{2,1,0:T(8,128)(2,1)}), bf16[4,96,768]{2,1,0:T(8,128)(2,1)}, u32[]{:S(2)}, u32[]{:S(2)}) async-start(bf16[4,96,768]{2,1,0:T(8,128)(2,1)} %pad_maximum_fusion.3), calls=%async_computation.10 | async-start | bytes 1179648 | tf_op jit(solution)/shard_map/all_to_all | solution.py:84
  290.9 7.9 %all-to-all-start.6 = ((f32[4,1,1152]{2,1,0:T(1,128)}), f32[4,1,1152]{2,1,0:T(1,128)S(1)}, u32[]{:S(2)}, u32[]{:S(2)}) async-start(f32[4,1,1152]{2,1,0:T(1,128)} %broadcast_in_dim.37), calls=%async_computation.8 | async-start | bytes 36864 | tf_op jit(solution)/shard_map/all_to_all | solution.py:84
  298.8 11.0 %all-to-all-start.9 = ((bf16[8,24,288]{2,1,0:T(8,128)(2,1)}), bf16[8,24,288]{2,1,0:T(8,128)(2,1)}, u32[]{:S(2)}, u32[]{:S(2)}) async-start(bf16[8,24,288]{2,1,0:T(8,128)(2,1)} %all_to_all.109), calls=%async_computation.11 | async-start | bytes 294912 | tf_op jit(solution)/shard_map/all_to_all | solution.py:84
  311.9 12.0 %all-to-all-start.10 = ((bf16[4,96,768]{2,1,0:T(8,128)(2,1)}), bf16[4,96,768]{2,1,0:T(8,128)(2,1)S(1)}, u32[]{:S(2)}, u32[]{:S(2)}) async-start(bf16[4,96,768]{2,1,0:T(8,128)(2,1)} %broadcast_in_dim.68), calls=%async_computation.12 | async-start | bytes 1179648 | tf_op jit(solution)/shard_map/all_to_all | solution.py:84
  (13 other events, 21.8 us)
Sparse Core Ops, SparseCore 0:
  10.3 54.3 all-gather.6
  72.3 23.8 all-gather.8
  97.9 33.6 all-gather.10
  143.9 33.5 reduce-scatter.2
  179.1 25.0 all-gather.14
  206.2 34.6 all-gather.12
  249.1 35.6 reduce-scatter.4
